TPU v7x, 32 devices: a whole 2x2x4 slice. The times are simulated.
32 devices in a mesh: group: 2 (over x), seq: 16 (over z, y, core).
Axes of the slice: x: 2, y: 2, z: 4, core: 2. Of those that a mesh axis runs over, the one named last changes fastest.
Arguments:
- queries: bfloat16 [8192, 768], P(('group', 'seq')), parts along dimension 0, may hold values from -6 to 6
- key_rows: bfloat16 [8192, 768], P(('group', 'seq')), parts along dimension 0, may hold values from -6 to 6
- value_rows: bfloat16 [8192, 768], P(('group', 'seq')), parts along dimension 0, may hold values from -20 to 20
- dilation: int32 [12], replicated, may hold values from 2 to 30, as said below
- global_rows: int32 [128], P('group'), parts along dimension 0, may hold values from 0 to 4095, as said below
- out_weight: bfloat16 [768, 1536], replicated, may hold values from -0.21875 to 0.21875
- mlp_up: bfloat16 [1536, 3072], P('seq'), may hold values from -0.15625 to 0.15625
- mlp_down: bfloat16 [3072, 1536], P('seq'), may hold values from -0.109375 to 0.109375
Outputs:
- attended: bfloat16 [8192, 1536], P(('group', 'seq')), parts along dimension 0
- mlp_out: bfloat16 [8192, 1536], P(('group', 'seq')), parts along dimension 0
There are 2 independent parts, one for each index of `group`. A program takes and returns all parts, laid end to end along the dimension named above; an argument that names none is the same for every part. Nothing has to cross between parts.
Inputs may be any that keep to these rules, and one draw needn't show every extreme that they name: `dilation`: each offset is a multiple of 2; some head has the smallest and some the largest. `global_rows`: distinct positions.
All inputs are finite; a program needn't handle non-finite values.
Results may differ from a plain program's by a relative error of at most 0.0071.
Values may be sent and summed in bfloat16 or wider, within the bound.
A program may use at most 192 MiB of HBM per device.

v0:
```python
import jax
import jax.numpy as jnp
from jax import lax
from jax.sharding import PartitionSpec as P

H = 12
DH = 64
BLK = 128
GLOBALS = 64


def with_halo(cells, sides, width):
    for axis, dim in sides:
        count = lax.axis_size(axis)
        head = lax.slice_in_dim(cells, 0, width, axis=dim)
        tail = lax.slice_in_dim(cells, cells.shape[dim] - width, cells.shape[dim], axis=dim)
        cells = jnp.concatenate(
            [
                lax.ppermute(tail, axis, [(i, (i + 1) % count) for i in range(count)]),
                cells,
                lax.ppermute(head, axis, [((i + 1) % count, i) for i in range(count)]),
            ],
            axis=dim,
        )
    return cells


def passed_along(value, axis, steps):
    count = lax.axis_size(axis)
    pairs = [(source, (source + steps) % count) for source in range(count)]
    return lax.ppermute(value, axis, pairs)


def merged_2(part, axis, combine):
    gathered = jax.tree.map(lambda a: lax.all_gather(a, axis), part)

    def take(source):
        return jax.tree.map(lambda a: lax.dynamic_index_in_dim(a, source, 0, False), gathered)

    return lax.fori_loop(
        1, lax.axis_size(axis), lambda source, state: combine(state, take(source)), take(0)
    )


def attend_blocks(query_blocks, local_keys, local_values, glob_keys, glob_values):
    count = query_blocks.shape[0]
    keys_all = jnp.concatenate(
        [local_keys, jnp.broadcast_to(glob_keys[None], (count,) + glob_keys.shape)], axis=1
    )
    values_all = jnp.concatenate(
        [local_values, jnp.broadcast_to(glob_values[None], (count,) + glob_values.shape)], axis=1
    )
    scores = jnp.einsum(
        "nqhd,nkhd->nhqk", query_blocks, keys_all, preferred_element_type=jnp.float32
    ) * DH ** (-0.5)
    peak = jnp.max(scores, axis=-1, keepdims=True)
    exp_terms = jnp.exp(scores - peak)
    totals = jnp.sum(exp_terms, axis=-1, keepdims=True)
    weights = (exp_terms / totals).astype(jnp.bfloat16)
    return jnp.einsum("nhqk,nkhd->nqhd", weights, values_all, preferred_element_type=jnp.float32)


def select_heads(chosen, arrived, current):
    shaped = current.shape
    head_mask = chosen[None, None, :, None]
    merged = jnp.where(
        head_mask,
        arrived.reshape(shaped[0], shaped[1], H, DH),
        current.reshape(shaped[0], shaped[1], H, DH),
    )
    return merged.reshape(shaped)


def join_partials(first, second):
    peak_first, total_first, numer_first = first
    peak_second, total_second, numer_second = second
    highest = jnp.maximum(peak_first, peak_second)
    scale_first = jnp.exp(peak_first - highest)
    scale_second = jnp.exp(peak_second - highest)
    return (
        highest,
        total_first * scale_first + total_second * scale_second,
        numer_first * scale_first[:, :, None] + numer_second * scale_second[:, :, None],
    )


def per_device(queries, key_rows, value_rows, dilation, global_rows, out_weight, mlp_up, mlp_down):
    tok_rows = queries.shape[0]
    blocks = tok_rows // BLK
    devices = lax.axis_size("seq")
    stacked = jnp.stack([key_rows, value_rows])
    padded = with_halo(stacked, (("seq", 1),), BLK)
    dev_hops = dilation // blocks
    current = stacked
    for bit_level in range((devices - 1).bit_length()):
        arrived = passed_along(current, "seq", -(1 << bit_level))
        chosen = dev_hops >> bit_level & 1 == 1
        current = select_heads(chosen, arrived, current)
    start = lax.axis_index("seq") * tok_rows
    offsets = global_rows - start
    onehot = offsets[:, None] == jnp.arange(tok_rows, dtype=jnp.int32)[None, :]
    picker = onehot.astype(jnp.bfloat16)
    picked = (
        jnp.dot(picker, queries, preferred_element_type=jnp.float32),
        jnp.dot(picker, key_rows, preferred_element_type=jnp.float32),
        jnp.dot(picker, value_rows, preferred_element_type=jnp.float32),
    )
    glob_q, glob_k, glob_v = lax.psum((picked[0], picked[1], picked[2]), "seq")
    glob_query = glob_q.astype(jnp.bfloat16).reshape(GLOBALS, H, DH)
    glob_keys = glob_k.astype(jnp.bfloat16).reshape(GLOBALS, H, DH)
    glob_values = glob_v.astype(jnp.bfloat16).reshape(GLOBALS, H, DH)
    grid = padded.reshape(2, blocks + 2, BLK, H, DH)
    dilated = current.reshape(2, blocks, BLK, H, DH)
    local_set = jnp.concatenate([grid[:, :-2], grid[:, 1:-1], grid[:, 2:], dilated], axis=2)
    attended_local = attend_blocks(
        queries.reshape(blocks, BLK, H, DH), local_set[0], local_set[1], glob_keys, glob_values
    ).reshape(tok_rows, H * DH)
    scores = jnp.einsum(
        "ghd,thd->hgt",
        glob_query,
        key_rows.reshape(tok_rows, H, DH),
        preferred_element_type=jnp.float32,
    ) * DH ** (-0.5)
    peak = jnp.max(scores, axis=2)
    exp_terms = jnp.exp(scores - peak[:, :, None])
    totals = jnp.sum(exp_terms, axis=2)
    numerators = jnp.einsum(
        "hgt,thd->hgd",
        exp_terms,
        value_rows.astype(jnp.float32).reshape(tok_rows, H, DH),
        precision=lax.Precision.HIGHEST,
    )
    peak, totals, numerators = merged_2((peak, totals, numerators), "seq", join_partials)
    glob_out = (numerators / totals[:, :, None]).transpose(1, 0, 2).reshape(GLOBALS, H * DH)
    onehot_float = onehot.astype(jnp.float32)
    placed = jnp.dot(onehot_float.T, glob_out, precision=lax.Precision.HIGHEST)
    owned_rows = jnp.sum(onehot_float, axis=0) > 0.5
    attention = jnp.where(owned_rows[:, None], placed, attended_local).astype(jnp.bfloat16)
    attended = jnp.dot(attention, out_weight, preferred_element_type=jnp.float32).astype(
        jnp.bfloat16
    )
    columns = attended
    pre_act = jnp.dot(
        columns,
        lax.all_gather(mlp_up, "seq", axis=0, tiled=True),
        preferred_element_type=jnp.float32,
    )
    hidden = jax.nn.gelu(pre_act, approximate=True).astype(jnp.bfloat16)
    columns = hidden
    mlp_out = jnp.dot(
        columns,
        lax.all_gather(mlp_down, "seq", axis=0, tiled=True),
        preferred_element_type=jnp.float32,
    ).astype(jnp.bfloat16)
    return (attended, mlp_out)


def solution(mesh):
    placed = (
        P(("group", "seq"), None),
        P(("group", "seq"), None),
        P(("group", "seq"), None),
        P(),
        P("group"),
        P(),
        P("seq", None),
        P("seq", None),
    )
    return jax.shard_map(
        per_device,
        mesh=mesh,
        in_specs=placed,
        out_specs=(P(("group", "seq"), None), P(("group", "seq"), None)),
        check_vma=False,
    )
```

profile of v0, /device:TPU:0, one launch (start us, length us, event | category | flops | bytes accessed | tf_op | source)
XLA Modules:
  0.0 397.6 jit_solution(10071234965016458596)
XLA Ops:
  7.2 1.3 copy.67
  9.2 1.9 fusion.47
  11.1 1.9 fusion.48
  13.0 2.0 copy.69
  15.0 2.0 fusion.49
  17.0 70.1 %all-reduce.2 = (bf16[64,768]{1,0:T(8,128)(2,1)}, bf16[64,768]{1,0:T(8,128)(2,1)}, bf16[64,768]{1,0:T(8,128)(2,1)}) all-reduce(f32[64,768]{1,0:T(8,128)} %fusion.47, f32[64,768]{1,0:T(8,128)} %fusion.48, f32[64,768]{1,0:T(8,128)} %fusion.49), channel_id=1, replica_groups=mesh['group'=2,'seq'=16] {'seq'}, use_global_device_ids=true, to_apply=%region_7.8 | all-reduce | flops 147456 | bytes 884736 | tf_op jit(solution)/shard_map/psum | solution.py:108
  87.1 1.8 reshape.87
  88.9 1.3 fusion.71
  91.1 2.4 fusion.37
  97.8 19.8 %collective-permute-done.2 = bf16[2,256,768]{2,1,0:T(8,128)(2,1)} collective-permute-done((bf16[2,256,768]{2,1,0:T(8,128)(2,1)}, bf16[2,256,768]{2,1,0:T(8,128)(2,1)}, u32[]{:S(2)}, u32[]{:S(2)}) %collective-permute-start.2) | collective-permute-done | bytes 786464 | tf_op jit(solution)/shard_map/ppermute | solution.py:31
  117.6 2.1 broadcast_select_fusion
  121.1 17.6 %collective-permute-done.3 = bf16[2,256,768]{2,1,0:T(8,128)(2,1)} collective-permute-done((bf16[2,256,768]{2,1,0:T(8,128)(2,1)}, bf16[2,256,768]{2,1,0:T(8,128)(2,1)}, u32[]{:S(2)}, u32[]{:S(2)}) %collective-permute-start.3) | collective-permute-done | bytes 786464 | tf_op jit(solution)/shard_map/ppermute | solution.py:31
  138.8 2.4 broadcast_select_fusion.1
  142.1 15.3 %collective-permute-start = (bf16[2,128,768]{2,1,0:T(8,128)(2,1)}, bf16[2,128,768]{2,1,0:T(8,128)(2,1)}, u32[]{:S(2)}, u32[]{:S(2)}) collective-permute-start(bf16[2,128,768]{2,1,0:T(8,128)(2,1)} %get-tuple-element.209), channel_id=1, source_target_pairs={{0,1},{1,2},{2,3},{3,4},{4,5},{5,6},{6,7},{7,8},{8,9},{9,10},{10,1... | collective-permute-start | bytes 1179656 | tf_op jit(solution)/shard_map/ppermute | solution.py:19
  157.4 4.5 %collective-permute-start.1 = (bf16[2,128,768]{2,1,0:T(8,128)(2,1)}, bf16[2,128,768]{2,1,0:T(8,128)(2,1)}, u32[]{:S(2)}, u32[]{:S(2)}) collective-permute-start(bf16[2,128,768]{2,1,0:T(8,128)(2,1)} %get-tuple-element.210), channel_id=1, source_target_pairs={{1,0},{2,1},{3,2},{4,3},{5,4},{6,5},{7,6},{8,7},{9,8},{10,9},{11,1... | collective-permute-start | bytes 1179656 | tf_op jit(solution)/shard_map/ppermute | solution.py:21
  162.7 1.9 stack.19
  164.6 2.0 copy.89
  167.3 1.1 copy.81
  168.4 1.8 copy.82
  170.2 1.7 copy.94
  171.9 1.8 reshape.96
  173.8 1.7 copy.93
  175.5 1.5 fusion.38
  176.9 23.6 %all-gather.4 = f32[16,12,64]{2,1,0:T(8,128)S(1)} all-gather(f32[1,12,64]{2,1,0:T(8,128)S(1)} %bitcast.103), channel_id=3, replica_groups=mesh['group'=2,'seq'=16] {'seq'}, dimensions={0}, use_global_device_ids=true | all-gather | bytes 52224 | tf_op jit(solution)/shard_map/all_gather | solution.py:35
  200.6 18.3 %all-gather.3 = f32[16,12,64]{2,1,0:T(8,128)S(1)} all-gather(f32[1,12,64]{2,1,0:T(8,128)S(1)} %bitcast.102), channel_id=2, replica_groups=mesh['group'=2,'seq'=16] {'seq'}, dimensions={0}, use_global_device_ids=true | all-gather | bytes 52224 | tf_op jit(solution)/shard_map/all_gather | solution.py:35
  219.5 2.4 broadcast_select_fusion.2
  222.5 2.4 pad_maximum_fusion.2
  224.9 2.6 copy.71
  227.5 3.5 reshape.91
  231.0 5.1 %fusion.65 = (bf16[2,2,128,12,64]{2,1,4,3,0:T(2,128)(2,1)S(1)}, bf16[2,2,128,12,64]{2,1,4,3,0:T(2,128)(2,1)S(1)}, bf16[2,2,128,12,64]{2,1,4,3,0:T(2,128)(2,1)S(1)}) fusion(bf16[2,4,128,12,64]{2,1,4,3,0:T(4,128)(2,1)} %reshape.91), kind=kLoop, calls=%fused_computation.98 | loop fusion | bytes 4718592 | tf_op jit(solution)/shard_map/slice | solution.py:114
  236.4 1.1 copy.96
  237.4 1.2 copy.97
  238.6 2.3 copy.78
  240.9 2.8 reshape.95
  243.7 2.3 copy.77
  246.0 2.7 reshape.94
  248.7 2.3 copy.76
  251.0 2.7 reshape.93
  253.7 39.6 %collective-permute-done.5 = bf16[2,256,768]{2,1,0:T(8,128)(2,1)} collective-permute-done((bf16[2,256,768]{2,1,0:T(8,128)(2,1)}, bf16[2,256,768]{2,1,0:T(8,128)(2,1)}, u32[]{:S(2)}, u32[]{:S(2)}) %collective-permute-start.5) | collective-permute-done | bytes 786464 | tf_op jit(solution)/shard_map/ppermute | solution.py:31
  293.3 2.3 copy.75
  295.6 2.7 reshape.92
  298.3 2.6 fusion.36
  301.6 1.9 slice_bitcast_fusion.1
  303.6 7.2 %fusion.66 = (f32[2,12,128]{2,1,0:T(8,128)S(1)}, f32[2,12,128,576]{2,3,1,0:T(8,128)}) fusion(bf16[2,64,12,64]{1,3,2,0:T(8,128)(2,1)S(1)} %broadcast_in_dim.97, bf16[2,512,12,64]{1,3,2,0:T(8,128)(2,1)} %get-tuple-element.205, bf16[2,128,12,64]{1,0,3,2:T(2,128)(2,1)S(1)} %copy-done.8), kind=kOutput, calls=%fused_computation.99 | convolution fusion | flops 235340352 | bytes 9252864 | tf_op jit(solution)/shard_map/sub | solution.py:57
  310.9 4.3 %fusion.30 = bf16[2,128,12,64]{1,3,2,0:T(8,128)(2,1)S(1)} fusion(f32[2,12,128,576]{2,3,1,0:T(8,128)} %get-tuple-element.215, f32[2,12,128]{2,1,0:T(8,128)S(1)} %get-tuple-element.214, bf16[2,64,12,64]{1,3,2,0:T(8,128)(2,1)S(1)} %broadcast_in_dim.95, bf16[2,512,12,64]{1,3,2,0:T(8,128)(2,1)} %get-tuple-element.204), kind=kOutput, calls=%fused_computation.42 | convolution fusion | flops 233570304 | bytes 9252864 | tf_op jit(solution)/shard_map/nhqk,nkhd->nqhd/dot_general | solution.py:60
  315.9 1.0 slice.38
  317.0 32.2 %while.19 = (s32[]{:T(128)}, f32[12,64]{1,0:T(8,128)S(1)}, f32[12,64]{1,0:T(8,128)S(1)}, f32[12,64,64]{2,1,0:T(8,128)S(1)}, f32[16,12,64]{2,1,0:T(8,128)}, /*ind...) while((s32[]{:T(128)}, f32[12,64]{1,0:T(8,128)S(1)}, ...), condition=%wide.region_5.6_spmd, body=%wide.region_4.5_spmd.sunk | while | flops 152069 | bytes 620695 | solution.py:40
  317.7 1.4 fusion.88
  319.8 1.4 fusion.88
  322.0 1.4 fusion.88
  324.1 1.4 fusion.88
  326.3 1.4 fusion.88
  328.4 1.4 fusion.88
  330.5 1.4 fusion.88
  332.7 1.5 fusion.88
  334.9 1.4 fusion.88
  337.1 1.4 fusion.88
  339.2 1.4 fusion.88
  341.4 1.4 fusion.88
  343.5 1.4 fusion.88
  345.6 1.4 fusion.88
  347.8 1.4 fusion.88
  351.2 27.4 %all-gather.9.cloned.1.call-done = bf16[1536,3072]{1,0:T(8,128)(2,1)} async-done(((bf16[96,3072]{1,0:T(8,128)(2,1)}), bf16[1536,3072]{1,0:T(8,128)(2,1)}) %all-gather.9.cloned.1.call-update) | async-done | bytes 9437200 | tf_op jit(solution)/shard_map/all_gather | solution.py:145
  378.6 12.4 %convolution_convert_fusion = bf16[256,1536]{1,0:T(8,128)(2,1)} fusion(bf16[3072,1536]{1,0:T(8,128)(2,1)} %all-gather.11.cloned.1.call-done, bf16[256,1536]{1,0:T(8,128)(2,1)S(1)} %convolution_convert_fusion.1, bf16[1536,3072]{1,0:T(8,128)(2,1)} %all-gather.9.cloned.1.call-done), kind=kOutput, calls=%fused_computation.28 | convolution fusion | flops 4839309312 | bytes 20447232 | tf_op jit(solution)/shard_map/dot_general | solution.py:150
  (96 shorter events, 25.7 us)
Async XLA Ops:
  7.2 343.2 %copy-start = (bf16[768,1536]{1,0:T(8,128)(2,1)S(1)}, bf16[768,1536]{1,0:T(8,128)(2,1)}, u32[]{:S(2)}) copy-start(bf16[768,1536]{1,0:T(8,128)(2,1)} %param.15) | copy-start | bytes 7077892
  7.2 308.7 %all-gather.13.cloned.1.call-start = ((), (), s32[]{:S(2)}) async-start(), calls=%async_computation.2 | async-start | bytes 6684672 | tf_op jit(solution)/shard_map/all_gather | solution.py:35
  9.2 79.7 %copy-start.11 = (s32[64]{0:T(128)}, s32[64]{0:T(128)S(1)}, u32[]{:S(2)}) copy-start(s32[64]{0:T(128)S(1)} %broadcast_subtract_fusion) | copy-start | bytes 772
  15.0 80.0 %copy-start.1 = (bf16[256,768]{1,0:T(8,128)(2,1)S(1)}, bf16[256,768]{1,0:T(8,128)(2,1)}, u32[]{:S(2)}) copy-start(bf16[256,768]{1,0:T(8,128)(2,1)} %param.11) | copy-start | bytes 1179652
  15.0 80.0 %copy-start.2 = (bf16[256,768]{1,0:T(8,128)(2,1)S(1)}, bf16[256,768]{1,0:T(8,128)(2,1)}, u32[]{:S(2)}) copy-start(bf16[256,768]{1,0:T(8,128)(2,1)} %param.12) | copy-start | bytes 1179652
  88.9 7.0 %copy-start.17 = (s32[12]{0:T(128)S(1)}, s32[12]{0:T(128)}, u32[]{:S(2)}) copy-start(s32[12]{0:T(128)} %param.13) | copy-start | bytes 148
  90.2 0.9 copy-start.3
  93.5 257.7 %all-gather.11.cloned.1.call-start = ((), (), s32[]{:S(2)}) async-start(), calls=%async_computation.1 | async-start | bytes 10027008 | tf_op jit(solution)/shard_map/all_gather | solution.py:152
  94.2 284.4 %all-gather.9.cloned.1.call-start = ((), (), s32[]{:S(2)}) async-start(), calls=%async_computation | async-start | bytes 10027008 | tf_op jit(solution)/shard_map/all_gather | solution.py:145
  95.9 21.7 %collective-permute-start.2 = (bf16[2,256,768]{2,1,0:T(8,128)(2,1)}, bf16[2,256,768]{2,1,0:T(8,128)(2,1)}, u32[]{:S(2)}, u32[]{:S(2)}) collective-permute-start(bf16[2,256,768]{2,1,0:T(8,128)(2,1)} %pad_maximum_fusion.9), channel_id=1, source_target_pairs={{0,15},{1,0},{2,1},{3,2},{4,3},{5,4},{6,5},{7,6},{8,7},{9,8},{10,9... | collective-permute-start | bytes 2359304 | tf_op jit(solution)/shard_map/ppermute | solution.py:31
  97.1 0.6 copy-start.15
  119.8 19.0 %collective-permute-start.3 = (bf16[2,256,768]{2,1,0:T(8,128)(2,1)}, bf16[2,256,768]{2,1,0:T(8,128)(2,1)}, u32[]{:S(2)}, u32[]{:S(2)}) collective-permute-start(bf16[2,256,768]{2,1,0:T(8,128)(2,1)} %broadcast_select_fusion), channel_id=1, source_target_pairs={{0,14},{1,15},{2,0},{3,1},{4,2},{5,3},{6,4},{7,5},{8,6},{9,7},{10,... | collective-permute-start | bytes 2359304 | tf_op jit(solution)/shard_map/ppermute | solution.py:31
  121.1 45.5 %copy-start.14 = (pred[12]{0:T(512)(128)(4,1)S(1)}, pred[12]{0:T(512)(128)(4,1)}, u32[]{:S(2)}) copy-start(pred[12]{0:T(512)(128)(4,1)} %get-tuple-element.211) | copy-start | bytes 40
  141.1 78.4 %collective-permute-start.4 = (bf16[2,256,768]{2,1,0:T(8,128)(2,1)}, bf16[2,256,768]{2,1,0:T(8,128)(2,1)}, u32[]{:S(2)}, u32[]{:S(2)}) collective-permute-start(bf16[2,256,768]{2,1,0:T(8,128)(2,1)} %broadcast_select_fusion.1), channel_id=1, source_target_pairs={{0,12},{1,13},{2,14},{3,15},{4,0},{5,1},{6,2},{7,3},{8,4},{9,5},{1... | collective-permute-start | bytes 2359304 | tf_op jit(solution)/shard_map/ppermute | solution.py:31
  142.1 80.4 %collective-permute-start = (bf16[2,128,768]{2,1,0:T(8,128)(2,1)}, bf16[2,128,768]{2,1,0:T(8,128)(2,1)}, u32[]{:S(2)}, u32[]{:S(2)}) collective-permute-start(bf16[2,128,768]{2,1,0:T(8,128)(2,1)} %get-tuple-element.209), channel_id=1, source_target_pairs={{0,1},{1,2},{2,3},{3,4},{4,5},{5,6},{6,7},{7,8},{8,9},{9,10},{10,1... | collective-permute-start | bytes 1179656 | tf_op jit(solution)/shard_map/ppermute | solution.py:19
  157.4 61.5 %copy-start.12 = (s32[64]{0:T(128)S(1)}, s32[64]{0:T(128)}, u32[]{:S(2)}) copy-start(s32[64]{0:T(128)} %copy-done.11) | copy-start | bytes 772
  157.4 65.1 %collective-permute-start.1 = (bf16[2,128,768]{2,1,0:T(8,128)(2,1)}, bf16[2,128,768]{2,1,0:T(8,128)(2,1)}, u32[]{:S(2)}, u32[]{:S(2)}) collective-permute-start(bf16[2,128,768]{2,1,0:T(8,128)(2,1)} %get-tuple-element.210), channel_id=1, source_target_pairs={{1,0},{2,1},{3,2},{4,3},{5,4},{6,5},{7,6},{8,7},{9,8},{10,9},{11,1... | collective-permute-start | bytes 1179656 | tf_op jit(solution)/shard_map/ppermute | solution.py:21
  200.6 18.4 %copy-start.9 = (f32[16,12,64]{2,1,0:T(8,128)}, f32[16,12,64]{2,1,0:T(8,128)S(1)}, u32[]{:S(2)}) copy-start(f32[16,12,64]{2,1,0:T(8,128)S(1)} %all-gather.4) | copy-start | bytes 147460
  218.8 0.7 copy-start.10
  221.9 71.4 %collective-permute-start.5 = (bf16[2,256,768]{2,1,0:T(8,128)(2,1)}, bf16[2,256,768]{2,1,0:T(8,128)(2,1)}, u32[]{:S(2)}, u32[]{:S(2)}) collective-permute-start(bf16[2,256,768]{2,1,0:T(8,128)(2,1)} %broadcast_select_fusion.2), channel_id=1, source_target_pairs={{0,8},{1,9},{2,10},{3,11},{4,12},{5,13},{6,14},{7,15},{8,0},{9,1},... | collective-permute-start | bytes 2359304 | tf_op jit(solution)/shard_map/ppermute | solution.py:31
  298.3 2.6 copy-start.4
  298.3 2.6 copy-start.5
  301.6 1.9 copy-start.7
  301.6 2.0 copy-start.8
  303.6 7.2 %copy-start.6 = (bf16[64,768]{0,1:T(8,128)(2,1)S(1)}, bf16[64,768]{0,1:T(8,128)(2,1)}, u32[]{:S(2)}) copy-start(bf16[64,768]{0,1:T(8,128)(2,1)} %copy.93) | copy-start | bytes 294916
  316.9 32.8 %copy-start.13 = (s32[64]{0:T(128)S(1)}, s32[64]{0:T(128)}, u32[]{:S(2)}) copy-start(s32[64]{0:T(128)} %copy-done.11) | copy-start | bytes 772
  316.9 32.8 %copy-start.16 = (pred[256]{0:T(512)(128)(4,1)S(1)}, pred[256]{0:T(512)(128)(4,1)}, u32[]{:S(2)}) copy-start(pred[256]{0:T(512)(128)(4,1)} %broadcast_compare_fusion) | copy-start | bytes 772
  351.1 39.9 %copy-start.18 = (bf16[256,1536]{1,0:T(8,128)(2,1)}, bf16[256,1536]{1,0:T(8,128)(2,1)S(1)}, u32[]{:S(2)}) copy-start(bf16[256,1536]{1,0:T(8,128)(2,1)S(1)} %convolution_convert_fusion.1) | copy-start | bytes 2359300
Sparse Core Ops, SparseCore 0:
  93.6 83.7 all-gather.12
  179.7 116.0 all-gather.10
  298.1 80.4 all-gather.8
where the time goes:
time: 400 us; the launch traced here: 398 us
  blocking collectives  112 us (28%)
  waiting for transfers between devices  106 us (26%)
  local copies, waits for them, and re-layouts  60.1 us (15%)
  other arithmetic  50.4 us (13%)
  matrix products  34.8 us (9%)
  starting transfers between devices  19.9 us (5%)
  between operations  14.1 us (4%)
    ppermute x4, waiting for transfers between devices, passed_along(): return lax.ppermute(value, axis, pairs)  77.1 us
    psum x1, blocking collectives, per_device(): glob_q, glob_k, glob_v = lax.psum((picked[0], picked[1], picked[2]), 'seq')  70.1 us
    all_gather x2, blocking collectives, merged_2(): gathered = jax.tree.map(lambda a: lax.all_gather(a, axis), part)  41.9 us
    all_gather x1, waiting for transfers between devices, per_device(): lax.all_gather(mlp_up, 'seq', axis=0, tiled=True)  27.4 us
    add x15, other arithmetic, join_partials(): numer_first * scale_first[:, :, None]  20.8 us
    ppermute x1, starting transfers between devices, with_halo(): lax.ppermute(tail, axis, [(i, (i + 1) % count) for i in range(count)])  15.3 us
    dot_general x1, matrix products, per_device(): jnp.dot(columns, lax.all_gather(mlp_down, 'seq', axis=0, tiled=True), pre...  12.4 us
    add x15, other arithmetic, join_partials(): total_first * scale_first + total_second * scale_second  11 us
  transfers between devices with their start and end apart: 9, of which 4 were waited for; matrix products, arithmetic and copies ran while one was open for 29% of the time, Pallas kernels for 0%

commit v1 on v0

--- a/solution.py
+++ b/solution.py
@@ -7,6 +7,27 @@
 DH = 64
 BLK = 128
 GLOBALS = 64
+
+
+def joined_along(blocks, dim):
+    blocks = jnp.moveaxis(blocks, 0, dim)
+    shape = blocks.shape
+    return blocks.reshape(*shape[:dim], shape[dim] * shape[dim + 1], *shape[dim + 2 :])
+
+
+def doubled(array, axis):
+    length, index = (lax.axis_size(axis), lax.axis_index(axis))
+    blocks, apart = (array[None], 1)
+    while apart < length:
+        other = lax.ppermute(blocks, axis, [(i, i ^ apart) for i in range(length)])
+        low = index & apart == 0
+        blocks = jnp.concatenate([jnp.where(low, blocks, other), jnp.where(low, other, blocks)])
+        apart *= 2
+    return blocks
+
+
+def doubled_up(shard, axis, dim):
+    return joined_along(doubled(shard, axis), dim)
 
 
 def with_halo(cells, sides, width):
@@ -140,11 +161,7 @@
         jnp.bfloat16
     )
     columns = attended
-    pre_act = jnp.dot(
-        columns,
-        lax.all_gather(mlp_up, "seq", axis=0, tiled=True),
-        preferred_element_type=jnp.float32,
-    )
+    pre_act = jnp.dot(columns, doubled_up(mlp_up, "seq", 0), preferred_element_type=jnp.float32)
     hidden = jax.nn.gelu(pre_act, approximate=True).astype(jnp.bfloat16)
     columns = hidden
     mlp_out = jnp.dot(

time: 400 us -> 566 us (1.42)
  waiting for transfers between devices: 106 us -> 263 us
  other arithmetic: 50.4 us -> 68.9 us
  starting transfers between devices: 19.9 us -> 10.2 us
    ppermute x0 -> x4, waiting for transfers between devices: none -> 182 us  [doubled(): other = lax.ppermute(blocks, axis, [(i, i ^ apart) for i in range(length)])]
    all_gather x1 -> x0, waiting for transfers between devices: 27.4 us -> none  [per_device(): lax.all_gather(mlp_up, 'seq', axis=0, tiled=True)]
    ppermute x1, starting transfers between devices: 15.3 us -> 0.51 us  [with_halo(): lax.ppermute(tail, axis, [(i, (i + 1) % count) for i in range(count)])]
    concatenate x0 -> x4, other arithmetic: none -> 9.68 us  [doubled(): jnp.concatenate([jnp.where(low, blocks, other), jnp.where(low, other, blo...]
    select_n x0 -> x4, other arithmetic: none -> 9.27 us  [doubled(): jnp.where(low, blocks, other)]
    unnamed x45 -> x59, local copies, waits for them, and re-layouts: 9.81 us -> 13 us
  transfers between devices with their start and end apart: 9 -> 12, of which waited for: 4 -> 5; matrix products, arithmetic and copies ran while one was open for 29% -> 24% of each run, Pallas kernels for 0% -> 0%
where the time goes in v1:
time: 566 us; the launch traced here: 563 us
  waiting for transfers between devices  263 us (46%)
  blocking collectives  108 us (19%)
  other arithmetic  68.9 us (12%)
  local copies, waits for them, and re-layouts  63.2 us (11%)
  matrix products  35.1 us (6%)
  between operations  14.4 us (3%)
  starting transfers between devices  10.2 us (2%)
    ppermute x4, waiting for transfers between devices, doubled(): other = lax.ppermute(blocks, axis, [(i, i ^ apart) for i in range(length)])  182 us
    ppermute x4, waiting for transfers between devices, passed_along(): return lax.ppermute(value, axis, pairs)  81.1 us
    psum x1, blocking collectives, per_device(): glob_q, glob_k, glob_v = lax.psum((picked[0], picked[1], picked[2]), 'seq')  70.1 us
    all_gather x2, blocking collectives, merged_2(): gathered = jax.tree.map(lambda a: lax.all_gather(a, axis), part)  37.9 us
    add x15, other arithmetic, join_partials(): numer_first * scale_first[:, :, None]  20.7 us
    unnamed x59, local copies, waits for them, and re-layouts  13 us
    dot_general x1, matrix products, per_device(): jnp.dot(columns, lax.all_gather(mlp_down, 'seq', axis=0, tiled=True), pre...  12.4 us
  transfers between devices with their start and end apart: 12, of which 5 were waited for; matrix products, arithmetic and copies ran while one was open for 24% of the time, Pallas kernels for 0%

profile of v1, /device:TPU:0, one launch (start us, length us, event | category | flops | bytes accessed | tf_op | source)
XLA Modules:
  0.0 563.3 jit_solution(5247173403233237808)
XLA Ops:
  7.2 1.3 copy.67
  9.2 1.9 fusion.47
  11.1 2.0 fusion.48
  13.1 1.9 copy.69
  15.0 1.9 fusion.49
  16.9 70.1 %all-reduce.2 = (bf16[64,768]{1,0:T(8,128)(2,1)}, bf16[64,768]{1,0:T(8,128)(2,1)}, bf16[64,768]{1,0:T(8,128)(2,1)}) all-reduce(f32[64,768]{1,0:T(8,128)} %fusion.47, f32[64,768]{1,0:T(8,128)} %fusion.48, f32[64,768]{1,0:T(8,128)} %fusion.49), channel_id=1, replica_groups=mesh['group'=2,'seq'=16] {'seq'}, use_global_device_ids=true, to_apply=%region_7.8 | all-reduce | flops 147456 | bytes 884736 | tf_op jit(solution)/shard_map/psum | solution.py:129
  87.1 1.8 reshape.90
  91.0 2.3 fusion.37
  96.0 3.9 collective-permute-start.1
  102.6 1.9 stack.19
  109.7 1.9 copy.81
  111.5 1.9 copy.82
  113.4 1.7 copy.94
  116.0 1.7 copy.93
  117.7 1.5 fusion.38
  119.2 18.2 %all-gather.4 = f32[16,12,64]{2,1,0:T(8,128)S(1)} all-gather(f32[1,12,64]{2,1,0:T(8,128)S(1)} %bitcast.109), channel_id=3, replica_groups=mesh['group'=2,'seq'=16] {'seq'}, dimensions={0}, use_global_device_ids=true | all-gather | bytes 52224 | tf_op jit(solution)/shard_map/all_gather | solution.py:56
  137.4 19.6 %all-gather.3 = f32[16,12,64]{2,1,0:T(8,128)S(1)} all-gather(f32[1,12,64]{2,1,0:T(8,128)S(1)} %bitcast.108), channel_id=2, replica_groups=mesh['group'=2,'seq'=16] {'seq'}, dimensions={0}, use_global_device_ids=true | all-gather | bytes 52224 | tf_op jit(solution)/shard_map/all_gather | solution.py:56
  161.7 1.9 collective-permute-start.7
  163.7 17.9 %collective-permute-done.3 = bf16[2,256,768]{2,1,0:T(8,128)(2,1)S(1)} collective-permute-done((bf16[2,256,768]{2,1,0:T(8,128)(2,1)S(1)}, bf16[2,256,768]{2,1,0:T(8,128)(2,1)S(1)}, u32[]{:S(2)}, u32[]{:S(2)}) %collective-permute-start.3) | collective-permute-done | bytes 786464 | tf_op jit(solution)/shard_map/ppermute | solution.py:52
  182.4 2.1 broadcast_select_fusion.7
  185.1 2.4 pad_maximum_fusion.5
  187.5 2.6 copy.71
  190.1 3.5 reshape.94
  193.6 5.0 fusion.65
  201.9 1.4 copy.78
  204.4 1.4 copy.77
  206.9 7.0 %collective-permute-done.4 = bf16[2,256,768]{2,1,0:T(8,128)(2,1)} collective-permute-done((bf16[2,256,768]{2,1,0:T(8,128)(2,1)}, bf16[2,256,768]{2,1,0:T(8,128)(2,1)}, u32[]{:S(2)}, u32[]{:S(2)}) %collective-permute-start.4) | collective-permute-done | bytes 786464 | tf_op jit(solution)/shard_map/ppermute | solution.py:52
  213.9 2.3 broadcast_select_fusion.8
  217.0 2.5 broadcast_select_fusion.5
  220.5 1.7 pad_maximum_fusion.3
  222.2 2.2 collective-permute-start.8
  224.4 2.3 copy.76
  226.7 2.7 reshape.96
  229.4 56.2 %collective-permute-done.5 = bf16[2,256,768]{2,1,0:T(8,128)(2,1)} collective-permute-done((bf16[2,256,768]{2,1,0:T(8,128)(2,1)}, bf16[2,256,768]{2,1,0:T(8,128)(2,1)}, u32[]{:S(2)}, u32[]{:S(2)}) %collective-permute-start.5) | collective-permute-done | bytes 786464 | tf_op jit(solution)/shard_map/ppermute | solution.py:52
  285.6 2.3 copy.75
  287.9 2.8 reshape.95
  290.7 2.7 fusion.36
  294.3 1.9 slice_bitcast_fusion.1
  297.1 7.7 %fusion.66 = (f32[2,12,128]{2,1,0:T(8,128)}, f32[2,12,128,576]{2,3,1,0:T(8,128)}) fusion(bf16[2,64,12,64]{1,3,2,0:T(8,128)(2,1)} %broadcast_in_dim.100, bf16[2,512,12,64]{1,3,2,0:T(8,128)(2,1)} %get-tuple-element.209, bf16[2,128,12,64]{1,0,3,2:T(2,128)(2,1)} %reshape.99), kind=kOutput, calls=%fused_computation.111 | convolution fusion | flops 235340352 | bytes 9252864 | tf_op jit(solution)/shard_map/sub | solution.py:78
  305.8 4.2 fusion.30
  311.2 1.9 copy.92
  313.2 12.1 %collective-permute-done.8 = bf16[4,96,3072]{2,1,0:T(8,128)(2,1)} collective-permute-done((bf16[4,96,3072]{2,1,0:T(8,128)(2,1)}, bf16[4,96,3072]{2,1,0:T(8,128)(2,1)}, u32[]{:S(2)}, u32[]{:S(2)}) %collective-permute-start.8) | collective-permute-done | bytes 2359328 | tf_op jit(solution)/shard_map/ppermute | solution.py:22
  325.2 2.3 broadcast_select_fusion.3
  327.5 2.9 pad_maximum_fusion.1
  332.6 32.1 %while.19 = (s32[]{:T(128)}, f32[12,64]{1,0:T(8,128)S(1)}, f32[12,64]{1,0:T(8,128)S(1)}, f32[12,64,64]{2,1,0:T(8,128)S(1)}, f32[16,12,64]{2,1,0:T(8,128)}, /*ind...) while((s32[]{:T(128)}, f32[12,64]{1,0:T(8,128)S(1)}, ...), condition=%wide.region_5.6_spmd, body=%wide.region_4.5_spmd.sunk | while | flops 152069 | bytes 620695 | solution.py:61
  333.4 1.4 fusion.88
  335.6 1.4 fusion.88
  337.7 1.4 fusion.88
  339.8 1.4 fusion.88
  342.0 1.4 fusion.88
  344.1 1.4 fusion.88
  346.3 1.4 fusion.88
  348.4 1.4 fusion.88
  350.5 1.4 fusion.88
  352.7 1.4 fusion.88
  354.8 1.4 fusion.88
  356.9 1.4 fusion.88
  359.1 1.4 fusion.88
  361.2 1.4 fusion.88
  363.3 1.4 fusion.88
  366.8 169.9 %collective-permute-done.9 = bf16[8,96,3072]{2,1,0:T(8,128)(2,1)} collective-permute-done((bf16[8,96,3072]{2,1,0:T(8,128)(2,1)}, bf16[8,96,3072]{2,1,0:T(8,128)(2,1)}, u32[]{:S(2)}, u32[]{:S(2)}) %collective-permute-start.9) | collective-permute-done | bytes 4718624 | tf_op jit(solution)/shard_map/ppermute | solution.py:22
  536.6 3.4 broadcast_select_fusion.1
  540.0 4.0 pad_maximum_fusion
  544.0 12.4 %convolution_convert_fusion = bf16[256,1536]{1,0:T(8,128)(2,1)} fusion(bf16[3072,1536]{1,0:T(8,128)(2,1)} %all-gather.8.cloned.1.call-done, bf16[256,1536]{1,0:T(8,128)(2,1)S(1)} %convolution_convert_fusion.1, bf16[1536,3072]{1,0:T(8,128)(2,1)} %bitcast.99), kind=kOutput, calls=%fused_computation.32 | convolution fusion | flops 4839309312 | bytes 20447232 | tf_op jit(solution)/shard_map/dot_general | solution.py:167
  (123 shorter events, 46.5 us)
Async XLA Ops:
  7.2 358.8 %copy-start = (bf16[768,1536]{1,0:T(8,128)(2,1)S(1)}, bf16[768,1536]{1,0:T(8,128)(2,1)}, u32[]{:S(2)}) copy-start(bf16[768,1536]{1,0:T(8,128)(2,1)} %param.15) | copy-start | bytes 7077892
  7.2 324.4 %all-gather.10.cloned.1.call-start = ((), (), s32[]{:S(2)}) async-start(), calls=%async_computation.1 | async-start | bytes 6684672 | tf_op jit(solution)/shard_map/all_gather | solution.py:56
  9.2 147.8 %copy-start.20 = (s32[64]{0:T(128)}, s32[64]{0:T(128)S(1)}, u32[]{:S(2)}) copy-start(s32[64]{0:T(128)S(1)} %broadcast_subtract_fusion) | copy-start | bytes 772
  11.1 82.4 %copy-start.4 = (bf16[256,768]{1,0:T(8,128)(2,1)S(1)}, bf16[256,768]{1,0:T(8,128)(2,1)}, u32[]{:S(2)}) copy-start(bf16[256,768]{1,0:T(8,128)(2,1)} %param.11) | copy-start | bytes 1179652
  11.1 82.4 %copy-start.5 = (bf16[256,768]{1,0:T(8,128)(2,1)S(1)}, bf16[256,768]{1,0:T(8,128)(2,1)}, u32[]{:S(2)}) copy-start(bf16[256,768]{1,0:T(8,128)(2,1)} %param.12) | copy-start | bytes 1179652
  90.2 0.9 copy-start.7
  93.4 450.6 %all-gather.8.cloned.1.call-start = ((), (), s32[]{:S(2)}) async-start(), calls=%async_computation | async-start | bytes 10027008 | tf_op jit(solution)/shard_map/all_gather | solution.py:169
  93.5 65.2 %collective-permute-start.6 = (bf16[1,96,3072]{2,1,0:T(8,128)(2,1)}, bf16[1,96,3072]{2,1,0:T(8,128)(2,1)}, u32[]{:S(2)}, u32[]{:S(2)}) collective-permute-start(bf16[1,96,3072]{2,1,0:T(8,128)(2,1)} %bitcast.107), channel_id=1, source_target_pairs={{0,1},{1,0},{2,3},{3,2},{4,5},{5,4},{6,7},{7,6},{8,9},{9,8},{10,11... | collective-permute-start | bytes 1769480 | tf_op jit(solution)/shard_map/ppermute | solution.py:22
  94.5 62.7 %collective-permute-start.2 = (bf16[2,256,768]{2,1,0:T(8,128)(2,1)}, bf16[2,256,768]{2,1,0:T(8,128)(2,1)}, u32[]{:S(2)}, u32[]{:S(2)}) collective-permute-start(bf16[2,256,768]{2,1,0:T(8,128)(2,1)} %pad_maximum_fusion.13), channel_id=1, source_target_pairs={{0,15},{1,0},{2,1},{3,2},{4,3},{5,4},{6,5},{7,6},{8,7},{9,8},{10,9... | collective-permute-start | bytes 2359304 | tf_op jit(solution)/shard_map/ppermute | solution.py:52
  95.5 89.6 %collective-permute-start = (bf16[2,128,768]{2,1,0:T(8,128)(2,1)}, bf16[2,128,768]{2,1,0:T(8,128)(2,1)}, u32[]{:S(2)}, u32[]{:S(2)}) collective-permute-start(bf16[2,128,768]{2,1,0:T(8,128)(2,1)} %get-tuple-element.217), channel_id=1, source_target_pairs={{0,1},{1,2},{2,3},{3,4},{4,5},{5,6},{6,7},{7,8},{8,9},{9,10},{10,1... | collective-permute-start | bytes 1179656 | tf_op jit(solution)/shard_map/ppermute | solution.py:40
  96.0 89.1 %collective-permute-start.1 = (bf16[2,128,768]{2,1,0:T(8,128)(2,1)}, bf16[2,128,768]{2,1,0:T(8,128)(2,1)}, u32[]{:S(2)}, u32[]{:S(2)}) collective-permute-start(bf16[2,128,768]{2,1,0:T(8,128)(2,1)} %get-tuple-element.218), channel_id=1, source_target_pairs={{1,0},{2,1},{3,2},{4,3},{5,4},{6,5},{7,6},{8,7},{9,8},{10,9},{11,1... | collective-permute-start | bytes 1179656 | tf_op jit(solution)/shard_map/ppermute | solution.py:42
  117.7 41.0 %copy-start.16 = (bf16[96,3072]{1,0:T(8,128)(2,1)S(1)}, bf16[96,3072]{1,0:T(8,128)(2,1)}, u32[]{:S(2)}) copy-start(bf16[96,3072]{1,0:T(8,128)(2,1)} %param.16) | copy-start | bytes 1769476
  137.4 24.3 %copy-start.17 = (f32[16,12,64]{2,1,0:T(8,128)}, f32[16,12,64]{2,1,0:T(8,128)S(1)}, u32[]{:S(2)}) copy-start(f32[16,12,64]{2,1,0:T(8,128)S(1)} %all-gather.4) | copy-start | bytes 147460
  157.0 4.7 copy-start.18
  157.2 25.2 %copy-start.19 = (pred[768]{0:T(1024)(128)(4,1)S(1)}, pred[768]{0:T(1024)(128)(4,1)}, u32[]{:S(2)}) copy-start(pred[768]{0:T(1024)(128)(4,1)} %broadcast_in_dim.92) | copy-start | bytes 2308
  157.2 25.2 %copy-start.23 = (pred[768]{0:T(1024)(128)(4,1)S(1)}, pred[768]{0:T(1024)(128)(4,1)}, u32[]{:S(2)}) copy-start(pred[768]{0:T(1024)(128)(4,1)} %broadcast_in_dim.89) | copy-start | bytes 2308
  158.4 23.1 %collective-permute-start.3 = (bf16[2,256,768]{2,1,0:T(8,128)(2,1)S(1)}, bf16[2,256,768]{2,1,0:T(8,128)(2,1)S(1)}, u32[]{:S(2)}, u32[]{:S(2)}) collective-permute-start(bf16[2,256,768]{2,1,0:T(8,128)(2,1)S(1)} %broadcast_select_fusion.6), channel_id=1, source_target_pairs={{0,14},{1,15},{2,0},{3,1},{4,2},{5,3},{6,4},{7,5},{8,6},{9,7},{10,... | collective-permute-start | bytes 2359304 | tf_op jit(solution)/shard_map/ppermute | solution.py:52
  159.8 0.8 copy-start.8
  159.8 1.9 copy-start.9
  161.7 55.3 %collective-permute-start.7 = (bf16[2,96,3072]{2,1,0:T(8,128)(2,1)}, bf16[2,96,3072]{2,1,0:T(8,128)(2,1)}, u32[]{:S(2)}, u32[]{:S(2)}) collective-permute-start(bf16[2,96,3072]{2,1,0:T(8,128)(2,1)} %pad_maximum_fusion.12), channel_id=1, source_target_pairs={{0,2},{1,3},{2,0},{3,1},{4,6},{5,7},{6,4},{7,5},{8,10},{9,11},{10,... | collective-permute-start | bytes 3538952 | tf_op jit(solution)/shard_map/ppermute | solution.py:22
  181.5 0.9 copy-start.13
  184.5 29.4 %collective-permute-start.4 = (bf16[2,256,768]{2,1,0:T(8,128)(2,1)}, bf16[2,256,768]{2,1,0:T(8,128)(2,1)}, u32[]{:S(2)}, u32[]{:S(2)}) collective-permute-start(bf16[2,256,768]{2,1,0:T(8,128)(2,1)} %broadcast_select_fusion.7), channel_id=1, source_target_pairs={{0,12},{1,13},{2,14},{3,15},{4,0},{5,1},{6,2},{7,3},{8,4},{9,5},{1... | collective-permute-start | bytes 2359304 | tf_op jit(solution)/shard_map/ppermute | solution.py:52
  201.9 12.0 %copy-start.22 = (pred[768]{0:T(1024)(128)(4,1)S(1)}, pred[768]{0:T(1024)(128)(4,1)}, u32[]{:S(2)}) copy-start(pred[768]{0:T(1024)(128)(4,1)} %broadcast_in_dim.86) | copy-start | bytes 2308
  216.2 69.4 %collective-permute-start.5 = (bf16[2,256,768]{2,1,0:T(8,128)(2,1)}, bf16[2,256,768]{2,1,0:T(8,128)(2,1)}, u32[]{:S(2)}, u32[]{:S(2)}) collective-permute-start(bf16[2,256,768]{2,1,0:T(8,128)(2,1)} %broadcast_select_fusion.8), channel_id=1, source_target_pairs={{0,8},{1,9},{2,10},{3,11},{4,12},{5,13},{6,14},{7,15},{8,0},{9,1},... | collective-permute-start | bytes 2359304 | tf_op jit(solution)/shard_map/ppermute | solution.py:52
  219.5 1.0 copy-start.6
  222.2 103.0 %collective-permute-start.8 = (bf16[4,96,3072]{2,1,0:T(8,128)(2,1)}, bf16[4,96,3072]{2,1,0:T(8,128)(2,1)}, u32[]{:S(2)}, u32[]{:S(2)}) collective-permute-start(bf16[4,96,3072]{2,1,0:T(8,128)(2,1)} %pad_maximum_fusion.3), channel_id=1, source_target_pairs={{0,4},{1,5},{2,6},{3,7},{4,0},{5,1},{6,2},{7,3},{8,12},{9,13},{10,... | collective-permute-start | bytes 7077896 | tf_op jit(solution)/shard_map/ppermute | solution.py:22
  290.7 2.7 copy-start.10
  290.7 2.8 copy-start.11
  290.7 2.9 copy-start.12
  294.3 2.0 copy-start.15
  327.5 2.9 copy-start.1
  327.5 3.6 copy-start.3
  331.1 205.5 %collective-permute-start.9 = (bf16[8,96,3072]{2,1,0:T(8,128)(2,1)}, bf16[8,96,3072]{2,1,0:T(8,128)(2,1)}, u32[]{:S(2)}, u32[]{:S(2)}) collective-permute-start(bf16[8,96,3072]{2,1,0:T(8,128)(2,1)} %pad_maximum_fusion.1), channel_id=1, source_target_pairs={{0,8},{1,9},{2,10},{3,11},{4,12},{5,13},{6,14},{7,15},{8,0},{9,1},... | collective-permute-start | bytes 14155784 | tf_op jit(solution)/shard_map/ppermute | solution.py:22
  332.6 32.7 %copy-start.14 = (bf16[256,768]{1,0:T(8,128)(2,1)S(1)}, bf16[256,768]{1,0:T(8,128)(2,1)}, u32[]{:S(2)}) copy-start(bf16[256,768]{1,0:T(8,128)(2,1)} %copy.92) | copy-start | bytes 1179652
  332.6 32.7 %copy-start.21 = (s32[64]{0:T(128)S(1)}, s32[64]{0:T(128)}, u32[]{:S(2)}) copy-start(s32[64]{0:T(128)} %copy-done.20) | copy-start | bytes 772
  332.6 32.7 %copy-start.24 = (pred[256]{0:T(512)(128)(4,1)S(1)}, pred[256]{0:T(512)(128)(4,1)}, u32[]{:S(2)}) copy-start(pred[256]{0:T(512)(128)(4,1)} %broadcast_compare_fusion) | copy-start | bytes 772
  365.3 171.3 %copy-start.2 = (bf16[4,96,3072]{2,1,0:T(8,128)(2,1)S(1)}, bf16[4,96,3072]{2,1,0:T(8,128)(2,1)}, u32[]{:S(2)}) copy-start(bf16[4,96,3072]{2,1,0:T(8,128)(2,1)} %copy-done.1) | copy-start | bytes 7077892
  366.7 177.3 %copy-start.25 = (bf16[256,1536]{1,0:T(8,128)(2,1)}, bf16[256,1536]{1,0:T(8,128)(2,1)S(1)}, u32[]{:S(2)}) copy-start(bf16[256,1536]{1,0:T(8,128)(2,1)S(1)} %convolution_convert_fusion.1) | copy-start | bytes 2359300
Sparse Core Ops, SparseCore 0:
  93.5 67.3 all-gather.9
  163.2 130.5 all-gather.7
